TPU v7x, 128 devices: a whole 4x4x4 slice. The times are simulated.
128 devices in a mesh: stream: 64 (over z, y, x), seq: 2 (over core).
Axes of the slice: x: 4, y: 4, z: 4, core: 2. Of those that a mesh axis runs over, the one named last changes fastest.
Arguments:
- head_inputs: bfloat16 [64, 3072, 1536], P('stream', 'seq'), may hold values from -6 to 6
- state_maps: bfloat16 [64, 3072, 256], P('stream', 'seq'), may hold values from -2.1 to 2.1
- step_logits: float32 [64, 24, 3072], P('stream', None, 'seq'), may hold values from -3 to 5.5
- log_rates: float32 [24], replicated, may hold values from -7 to 0
- step_bias: float32 [24], replicated, may hold values from -6 to -2
- skip_gain: float32 [24], replicated, may hold values from 0.25 to 1.75
- old_states: float32 [64, 24, 64, 128], P('stream', 'seq'), may hold values from -6 to 6
- old_owner: int32 [64], replicated, may hold values from 0 to 63, as said below
- doc_starts: int32 [64, 2], P('stream'), may hold values from 0 to 3071
- grad_output: bfloat16 [64, 3072, 1536], P('stream', 'seq'), may hold values from -6 to 6
Outputs:
- layer_out: bfloat16 [64, 3072, 1536], P('stream', 'seq')
- grad_inputs: bfloat16 [64, 3072, 1536], P('stream', 'seq')
- grad_maps: bfloat16 [64, 3072, 256], P('stream', 'seq')
- grad_logits: float32 [64, 24, 3072], P('stream', None, 'seq')
- grad_rates: float32 [24], replicated
- grad_bias: float32 [24], replicated
- grad_skip: float32 [24], replicated
Inputs may be any that keep to these rules, and one draw needn't show every extreme that they name: A permutation of the 64 stream indices: new stream s continues old stream old_owner[s]. `doc_starts`: positions in a stream's segment where a document starts and the state is cleared; entries may repeat.
All inputs are finite; a program needn't handle non-finite values.
Results may differ from a plain program's by a relative error of at most 0.013.
Values sent between devices are 32-bit elements; how exact they have to be, the bound alone decides.
No kernel may reach another device: no remote copies, remote signals or barrier semaphores. Data moves between devices by JAX's collectives and lax.ppermute only.
A program may use at most 192 MiB of HBM per device.

v0:
```python
import jax
import jax.numpy as jnp
from jax import lax
from jax.sharding import PartitionSpec as P

GROUP = 256


def shifted_2(shard, axis, by):
    size = lax.axis_size(axis)
    pairs = [(i, i + by) for i in range(size) if 0 <= i + by < size]
    return lax.ppermute(shard, axis, pairs)


def decay_terms(logits_part, flags_part, log_rates, step_bias):
    step_size = jax.nn.softplus(logits_part + step_bias[:, None])
    cum_decay = jnp.cumsum(-step_size * jnp.exp(log_rates)[:, None], axis=-1)
    doc_index = jnp.cumsum(flags_part, axis=-1)
    return (step_size, cum_decay, doc_index)


def group_states(inputs_c, maps_c, logits_c, flags_c, log_rates, step_bias):
    step_size, cum_decay, doc_index = decay_terms(logits_c, flags_c, log_rates, step_bias)
    state_n = maps_c.shape[-1] // 2
    b_part = maps_c[:, :, :state_n].astype(jnp.float32)
    same_doc = doc_index == doc_index[:, -1:]
    weight = (
        jnp.where(same_doc[:, None, :], jnp.exp(cum_decay[:, :, -1:] - cum_decay), 0.0) * step_size
    )
    b_weighted = (weight[:, :, :, None] * b_part[:, None, :, :]).astype(jnp.bfloat16)
    states = jnp.einsum("cjhp,chjn->chpn", inputs_c, b_weighted, preferred_element_type=jnp.float32)
    decays = jnp.where(doc_index[:, -1:] == 0, jnp.exp(cum_decay[:, :, -1]), 0.0)
    return (states, decays)


def group_inputs(start_state, states, decays):

    def advance(carry, members):
        group_state, group_decay = members
        return (group_decay[:, None, None] * carry + group_state, carry)

    return lax.scan(advance, start_state, (states, decays))


def one_group(inputs_q, maps_q, logits_q, flags_q, starts_q, log_rates, step_bias, skip_gain):
    step_size, cum_decay, doc_index = decay_terms(logits_q, flags_q, log_rates, step_bias)
    state_n = maps_q.shape[-1] // 2
    b_part = maps_q[:, :state_n]
    c_part = maps_q[:, state_n:]
    scores = jnp.dot(c_part, b_part.T, preferred_element_type=jnp.float32)
    position = jnp.arange(maps_q.shape[0])
    visible = (position[None, :] <= position[:, None]) & (doc_index[None, :] == doc_index[:, None])
    log_gaps = jnp.where(visible[None], cum_decay[:, :, None] - cum_decay[:, None, :], -jnp.inf)
    mixing = (scores[None] * jnp.exp(log_gaps) * step_size[:, None, :]).astype(jnp.bfloat16)
    local_part = jnp.einsum("hij,jhp->ihp", mixing, inputs_q, preferred_element_type=jnp.float32)
    inflow = jnp.where(doc_index[None, :] == 0, jnp.exp(cum_decay), 0.0)
    carried = jnp.einsum(
        "in,hpn->ihp", c_part.astype(jnp.float32), starts_q, precision=lax.Precision.HIGHEST
    )
    summed = (
        local_part
        + carried * inflow.T[:, :, None]
        + skip_gain[None, :, None] * inputs_q.astype(jnp.float32)
    )
    return summed.reshape(inputs_q.shape[0], -1).astype(jnp.bfloat16)


def outputs(inputs_c, maps_c, logits_c, flags_c, log_rates, step_bias, skip_gain, starts_c):

    def per_group(carry, members):
        inputs_q, maps_q, logits_q, flags_q, starts_q = members
        return (
            carry,
            jax.checkpoint(one_group)(
                inputs_q, maps_q, logits_q, flags_q, starts_q, log_rates, step_bias, skip_gain
            ),
        )

    _, result = lax.scan(per_group, 0, (inputs_c, maps_c, logits_c, flags_c, starts_c))
    return result


def shards(
    head_inputs,
    state_maps,
    step_logits,
    log_rates,
    step_bias,
    skip_gain,
    old_states,
    old_owner,
    doc_starts,
    grad_output,
):
    length = head_inputs.shape[1]
    head_count = step_logits.shape[1]
    head_dim = old_states.shape[2]
    state_n = old_states.shape[3]
    groups = length // GROUP
    seq_index = lax.axis_index("seq")
    stream_index = lax.axis_index("stream")
    position = seq_index * length + lax.iota(jnp.int32, length)
    reset_flags = jnp.any(doc_starts[0][:, None] == position[None, :], axis=0).astype(jnp.int32)
    gathered = lax.all_gather(old_states, "stream", axis=0, tiled=True)
    own_block = lax.dynamic_index_in_dim(gathered, old_owner[stream_index], 0, keepdims=False)
    start_state = lax.all_gather(own_block, "seq", axis=0, tiled=True)
    inputs_c = head_inputs[0].reshape(groups, GROUP, head_count, head_dim)
    maps_c = state_maps[0].reshape(groups, GROUP, 2 * state_n)
    logits_c = step_logits[0].reshape(head_count, groups, GROUP).transpose(1, 0, 2)
    flags_c = reset_flags.reshape(groups, GROUP)

    def state_part(inputs_c, maps_c, logits_c, log_rates, step_bias):
        return group_states(inputs_c, maps_c, logits_c, flags_c, log_rates, step_bias)

    (states, decays), pull_states = jax.vjp(
        state_part, inputs_c, maps_c, logits_c, log_rates, step_bias
    )
    empty_state = jnp.zeros((head_count, head_dim, state_n), jnp.float32)
    local_state, _ = group_inputs(empty_state, states, decays)
    shard_decay = jnp.prod(decays, axis=0)
    is_first = seq_index == 0

    def forward_turn(counter, entering):
        leaving = shard_decay[:, None, None] * entering + local_state
        shifted = shifted_2(leaving, "seq", 1)
        return jnp.where(is_first, start_state, shifted)

    entry_state = lax.fori_loop(0, lax.axis_size("seq") - 1, forward_turn, start_state)
    (exit_state, starts_c), pull_inputs = jax.vjp(group_inputs, entry_state, states, decays)

    def output_part(inputs_c, maps_c, logits_c, log_rates, step_bias, skip_gain, starts_c):
        return outputs(
            inputs_c, maps_c, logits_c, flags_c, log_rates, step_bias, skip_gain, starts_c
        )

    result, pull_output = jax.vjp(
        output_part, inputs_c, maps_c, logits_c, log_rates, step_bias, skip_gain, starts_c
    )
    grads_c = grad_output[0].reshape(groups, GROUP, head_count * head_dim)
    in_first, maps_first, logits_first, rates_first, bias_first, skip_total, grad_starts = (
        pull_output(grads_c)
    )
    from_output = pull_inputs((jnp.zeros_like(exit_state), grad_starts))[0]

    def backward_turn(counter, leaving_grad):
        entering_grad = shard_decay[:, None, None] * leaving_grad + from_output
        return shifted_2(entering_grad, "seq", -1)

    exit_grad = lax.fori_loop(0, lax.axis_size("seq") - 1, backward_turn, empty_state)
    _, grad_states, grad_decays = pull_inputs((exit_grad, grad_starts))
    in_second, maps_second, logits_second, rates_second, bias_second = pull_states(
        (grad_states, grad_decays)
    )
    rates_total, bias_total, skip_sum = lax.psum(
        (rates_first + rates_second, bias_first + bias_second, skip_total), ("stream", "seq")
    )
    grad_logits = (logits_first + logits_second).transpose(1, 0, 2).reshape(1, head_count, length)
    return (
        result.reshape(1, length, -1),
        (in_first + in_second).reshape(1, length, -1),
        (maps_first + maps_second).reshape(1, length, -1),
        grad_logits,
        rates_total,
        bias_total,
        skip_sum,
    )


def solution(mesh):
    return jax.shard_map(
        shards,
        mesh=mesh,
        in_specs=(
            P("stream", "seq", None),
            P("stream", "seq", None),
            P("stream", None, "seq"),
            P(),
            P(),
            P(),
            P("stream", "seq", None, None),
            P(),
            P("stream", None),
            P("stream", "seq", None),
        ),
        out_specs=(
            P("stream", "seq", None),
            P("stream", "seq", None),
            P("stream", "seq", None),
            P("stream", None, "seq"),
            P(),
            P(),
            P(),
        ),
        check_vma=False,
    )
```

profile of v0, /device:TPU:1, one launch (start us, length us, event | category | flops | bytes accessed | tf_op | source)
XLA Modules:
  0.0 601.4 jit_solution(6530939128043399756)
XLA Ops:
  21.2 12.9 %reshape.634 = bf16[6,256,24,64]{3,2,1,0:T(8,128)(2,1)} reshape(bf16[1,1536,1536]{2,1,0:T(8,128)(2,1)} %param.22) | data formatting | bytes 9437184 | tf_op jit(solution)/shard_map/reshape;squeeze | solution.py:107
  34.1 10.3 %copy.231 = bf16[6,256,24,64]{1,3,2,0:T(8,128)(2,1)} copy(bf16[6,256,24,64]{3,2,1,0:T(8,128)(2,1)} %reshape.634) | data formatting | bytes 9437184
  46.2 8.0 %fusion.94 = f32[6,24,64,128]{3,2,1,0:T(8,128)} fusion(bf16[6,256,24,64]{1,3,2,0:T(8,128)(2,1)} %copy.231, f32[6,256,128]{1,2,0:T(8,128)S(1)} %copy.228, f32[6,24,256]{2,1,0:T(8,128)S(1)} %select_multiply_fusion.3), kind=kOutput, calls=%fused_computation.172 | convolution fusion | flops 613416960 | bytes 10371072 | tf_op jit(solution)/shard_map/jvp(cjhp,chjn->chpn)/dot_general | solution.py:31
  54.2 8.2 %while.108 = (s32[]{:T(128)}, f32[24,64,128]{2,1,0:T(8,128)S(1)}, f32[6,24]{1,0:T(8,128)S(1)}, f32[6,24,64,128]{3,2,1,0:T(8,128)}, s32[]{:T(128)}, /*index=5*/s32[]{:T(128)}) while((s32[]{:T(128)}, f32[24,64,128]{2,1,0:T(8,128)S(1)}, f32[6,24]{1,0:T(8,128)S(1)}, f32[6,24,64,128]{3,2,1,0:T(8,128)}, s32[]{:T(128)}, ...), condition=%wide.region_7.8_spmd.clone, body=%wide.region_6.7_spmd.clone.sunk | while | flops 589827 | bytes 2359671 | solution.py:42
  62.4 83.2 %all-gather.3.cloned.1.call-done = f32[64,12,64,128]{3,2,1,0:T(8,128)} async-done(((f32[1,12,64,128]{3,2,1,0:T(8,128)}), f32[64,12,64,128]{3,2,1,0:T(8,128)}) %all-gather.3.cloned.1.call-update) | async-done | bytes 25165840 | tf_op jit(solution)/shard_map/all_gather | solution.py:104
  157.7 17.0 %while.105 = (s32[]{:T(128)}, f32[24,64,128]{2,1,0:T(8,128)S(1)}, f32[6,24,64,128]{3,2,1,0:T(8,128)}, f32[6,24,1,1]{1,3,2,0:T(1,128)}, f32[6,24]{1,0:T(8,128)S(1)}, /*index=5*/f32[6,24,64,128]{3,2,1,0:T(8,128)}, s32[]{:T(128)}) while((s32[]{:T(128)}, f32[24,64,128]{2,1,0:T(8,128)S(1)}, f32[6,24,64,128]{3,2,1,0:T(8,128)}, ...), condition=%wide.region_9.10_spmd, body=%wide.region_8.9_spmd.sunk | while | flops 393218 | bytes 3934165 | solution.py:42
  181.7 195.7 %while.109 = (s32[]{:T(128)}, f32[24]{0:T(128)}, f32[24]{0:T(128)}, f32[24]{0:T(128)}, bf16[6,256,24,64]{1,3,2,0:T(8,128)(2,1)}, /*index=5*/bf16[6,256,256]{1,2,...) while((s32[]{:T(128)}, f32[24]{0:T(128)}, f32[24]{0:T(128)}, ...), condition=%wide.region_31.32_spmd.clone, body=%wide.region_16.31_spmd.clone.sunk | while | flops 2306163200 | bytes 22004424 | solution.py:79
  193.2 6.2 %fusion.183 = (f32[24,256]{1,0:T(8,128)S(1)}, f32[24,256]{1,0:T(8,128)S(1)}, f32[24,256]{1,0:T(8,128)}, bf16[256,256]{1,0:T(8,128)(2,1)S(1)}) fusion(f32[24,256]{1,0:T(8,128)S(1)} %copy_bitcast_fusion.13, f32[24,256]{1,0:T(8,128)} %get-tuple-element.1559, f32[256,256]{1,0:T(8,128)S(1)} %fusion.181, pred[256,256]{1,0:T(8,128)(4,1)S(1)} %fusion.182, ...), kind=kOutput, calls=%fused_computation.73.clone.1 | convolution fusion | flops 224835584 | bytes 2154496 | tf_op jit(solution)/shard_map/transpose(jvp())/while/body/eval_jaxpr/checkpoint/hij,jhp->ihp/dot_general | solution.py:55
  205.2 3.9 fusion.189
  225.8 6.2 %fusion.183 = (f32[24,256]{1,0:T(8,128)S(1)}, f32[24,256]{1,0:T(8,128)S(1)}, f32[24,256]{1,0:T(8,128)}, bf16[256,256]{1,0:T(8,128)(2,1)S(1)}) fusion(f32[24,256]{1,0:T(8,128)S(1)} %copy_bitcast_fusion.13, f32[24,256]{1,0:T(8,128)} %get-tuple-element.1559, f32[256,256]{1,0:T(8,128)S(1)} %fusion.181, pred[256,256]{1,0:T(8,128)(4,1)S(1)} %fusion.182, ...), kind=kOutput, calls=%fused_computation.73.clone.1 | convolution fusion | flops 224835584 | bytes 2154496 | tf_op jit(solution)/shard_map/transpose(jvp())/while/body/eval_jaxpr/checkpoint/hij,jhp->ihp/dot_general | solution.py:55
  237.8 3.9 fusion.189
  258.4 6.2 %fusion.183 = (f32[24,256]{1,0:T(8,128)S(1)}, f32[24,256]{1,0:T(8,128)S(1)}, f32[24,256]{1,0:T(8,128)}, bf16[256,256]{1,0:T(8,128)(2,1)S(1)}) fusion(f32[24,256]{1,0:T(8,128)S(1)} %copy_bitcast_fusion.13, f32[24,256]{1,0:T(8,128)} %get-tuple-element.1559, f32[256,256]{1,0:T(8,128)S(1)} %fusion.181, pred[256,256]{1,0:T(8,128)(4,1)S(1)} %fusion.182, ...), kind=kOutput, calls=%fused_computation.73.clone.1 | convolution fusion | flops 224835584 | bytes 2154496 | tf_op jit(solution)/shard_map/transpose(jvp())/while/body/eval_jaxpr/checkpoint/hij,jhp->ihp/dot_general | solution.py:55
  270.4 3.9 fusion.189
  291.0 6.2 %fusion.183 = (f32[24,256]{1,0:T(8,128)S(1)}, f32[24,256]{1,0:T(8,128)S(1)}, f32[24,256]{1,0:T(8,128)}, bf16[256,256]{1,0:T(8,128)(2,1)S(1)}) fusion(f32[24,256]{1,0:T(8,128)S(1)} %copy_bitcast_fusion.13, f32[24,256]{1,0:T(8,128)} %get-tuple-element.1559, f32[256,256]{1,0:T(8,128)S(1)} %fusion.181, pred[256,256]{1,0:T(8,128)(4,1)S(1)} %fusion.182, ...), kind=kOutput, calls=%fused_computation.73.clone.1 | convolution fusion | flops 224835584 | bytes 2154496 | tf_op jit(solution)/shard_map/transpose(jvp())/while/body/eval_jaxpr/checkpoint/hij,jhp->ihp/dot_general | solution.py:55
  303.0 3.9 fusion.189
  323.7 6.2 %fusion.183 = (f32[24,256]{1,0:T(8,128)S(1)}, f32[24,256]{1,0:T(8,128)S(1)}, f32[24,256]{1,0:T(8,128)}, bf16[256,256]{1,0:T(8,128)(2,1)S(1)}) fusion(f32[24,256]{1,0:T(8,128)S(1)} %copy_bitcast_fusion.13, f32[24,256]{1,0:T(8,128)} %get-tuple-element.1559, f32[256,256]{1,0:T(8,128)S(1)} %fusion.181, pred[256,256]{1,0:T(8,128)(4,1)S(1)} %fusion.182, ...), kind=kOutput, calls=%fused_computation.73.clone.1 | convolution fusion | flops 224835584 | bytes 2154496 | tf_op jit(solution)/shard_map/transpose(jvp())/while/body/eval_jaxpr/checkpoint/hij,jhp->ihp/dot_general | solution.py:55
  335.7 3.9 fusion.189
  356.3 6.2 %fusion.183 = (f32[24,256]{1,0:T(8,128)S(1)}, f32[24,256]{1,0:T(8,128)S(1)}, f32[24,256]{1,0:T(8,128)}, bf16[256,256]{1,0:T(8,128)(2,1)S(1)}) fusion(f32[24,256]{1,0:T(8,128)S(1)} %copy_bitcast_fusion.13, f32[24,256]{1,0:T(8,128)} %get-tuple-element.1559, f32[256,256]{1,0:T(8,128)S(1)} %fusion.181, pred[256,256]{1,0:T(8,128)(4,1)S(1)} %fusion.182, ...), kind=kOutput, calls=%fused_computation.73.clone.1 | convolution fusion | flops 224835584 | bytes 2154496 | tf_op jit(solution)/shard_map/transpose(jvp())/while/body/eval_jaxpr/checkpoint/hij,jhp->ihp/dot_general | solution.py:55
  368.3 3.9 fusion.189
  377.5 11.6 %while.110 = (s32[]{:T(128)}, f32[24,64,128]{2,1,0:T(8,128)S(1)}, f32[6,24,64,128]{3,2,1,0:T(8,128)}, f32[6,24,1,1]{1,3,2,0:T(1,128)}, s32[]{:T(128)}, /*index=5*/s32[]{:T(128)}, s32[]{:T(128)}) while((s32[]{:T(128)}, f32[24,64,128]{2,1,0:T(8,128)S(1)}, f32[6,24,64,128]{3,2,1,0:T(8,128)}, f32[6,24,1,1]{1,3,2,0:T(1,128)}, ...), condition=%wide.region_33.34_spmd.clone, body=%wide.region_32.33_spmd.clone.sunk | while | flops 589828 | bytes 2359691 | solution.py:42
  394.3 15.2 %while.106 = (s32[]{:T(128)}, f32[24,64,128]{2,1,0:T(8,128)S(1)}, bf16[6,24,64,128]{3,2,1,0:T(8,128)(2,1)S(1)}, f32[6,24]{1,0:T(8,128)S(1)}, f32[6,24,64,128]{3,...) while((s32[]{:T(128)}, f32[24,64,128]{2,1,0:T(8,128)S(1)}, ...), condition=%wide.region_36.37_spmd, body=%wide.region_34.36_spmd.sunk | while | flops 786411 | bytes 4719297 | solution.py:42
  410.9 7.1 %fusion.87 = (f32[6,24,256]{2,1,0:T(8,128)S(1)}, bf16[6,256,128]{1,2,0:T(8,128)(2,1)S(1)}) fusion(f32[6,256,128]{1,2,0:T(8,128)} %copy-done.6, f32[6,24,256]{2,1,0:T(8,128)S(1)} %copy-done.16, bf16[6,24,64,128]{3,2,1,0:T(8,128)(2,1)} %copy-done.4, bf16[6,256,24,64]{1,3,2,0:T(8,128)(2,1)} %get-tuple-element.1777), kind=kOutput, calls=%fused_computation.162 | convolution fusion | flops 627339264 | bytes 8552448 | tf_op jit(solution)/shard_map/transpose(jvp(cjhp,chjn->chpn))/dot_general | solution.py:31
  418.8 14.9 %reduce-window.130 = f32[6,24,2,128]{3,1,2,0:T(8,128)S(1)} reduce-window(f32[6,24,2,128]{3,1,2,0:T(8,128)S(1)} %copy_bitcast_fusion.5, f32[]{:T(128)} %constant.289.clone.1), window={size=1x1x1x128 pad=0_0x0_0x0_0x0_127}, to_apply=%region_40.41 | reduce-window | flops 4681728 | bytes 294916 | tf_op jit(solution)/shard_map/reduce-window.14
  436.3 6.9 %bitcast_add_fusion.6 = bf16[6,256,24,64]{1,3,2,0:T(8,128)(2,1)} fusion(bf16[6,256,24,64]{1,3,2,0:T(8,128)(2,1)} %get-tuple-element.766, bf16[6,24,64,128]{3,2,1,0:T(8,128)(2,1)} %copy-done.4, f32[6,256,128]{1,2,0:T(8,128)S(1)} %copy-done.7, f32[6,24,256]{2,1,0:T(8,128)S(1)} %copy-done.16), kind=kOutput, calls=%fused_computation.171 | convolution fusion | flops 615776256 | bytes 12730368 | tf_op jit(solution)/shard_map/transpose(jvp(cjhp,chjn->chpn))/dot_general | solution.py:31
  443.2 10.4 %copy.250 = bf16[6,256,24,64]{3,2,1,0:T(8,128)(2,1)} copy(bf16[6,256,24,64]{1,3,2,0:T(8,128)(2,1)} %bitcast_add_fusion.6) | data formatting | bytes 9437184
  453.6 13.1 %reshape.633 = bf16[1,1536,1536]{2,1,0:T(8,128)(2,1)} reshape(bf16[6,256,24,64]{3,2,1,0:T(8,128)(2,1)} %copy.250) | data formatting | bytes 9437184
  467.4 62.6 %while.107 = (s32[]{:T(128)}, bf16[6,256,1536]{2,1,0:T(8,128)(2,1)}, bf16[6,256,24,64]{1,3,2,0:T(8,128)(2,1)}, bf16[6,256,256]{2,1,0:T(8,128)(2,1)}, s32[6,256]{...) while((s32[]{:T(128)}, bf16[6,256,1536]{2,1,0:T(8,128)(2,1)}, ...), condition=%wide.region_15.16_spmd.clone, body=%wide.region_10.15_spmd.clone.sunk | while | flops 833433920 | bytes 10981461 | solution.py:79
  473.3 3.5 fusion.167
  494.0 3.6 fusion.167
  514.8 3.6 fusion.167
  525.2 3.5 fusion.167
  530.0 64.5 %all-reduce.5 = (f32[24]{0:T(128)}, f32[24]{0:T(128)}, f32[24]{0:T(128)}) all-reduce(f32[24]{0:T(128)S(1)} %get-tuple-element.1226, f32[24]{0:T(128)S(1)} %add.228, f32[24]{0:T(128)S(1)} %copy-done.26), channel_id=1, replica_groups=mesh['stream'=64,'seq'=2] {'stream','seq'}, use_global_device_ids=true, to_apply=%region_43.44 | all-reduce | flops 72 | bytes 576 | tf_op jit(solution)/shard_map/psum | solution.py:154
  (709 shorter events, 276.4 us)
Async XLA Ops:
  7.2 138.5 %all-gather.3.cloned.1.call-start = ((), (), s32[]{:S(2)}) async-start(), calls=%async_computation | async-start | bytes 25559040 | tf_op jit(solution)/shard_map/all_gather | solution.py:104
  14.3 19.8 %copy-start.32 = (f32[24]{0:T(128)}, f32[24]{0:T(128)S(1)}, u32[]{:S(2)}) copy-start(f32[24]{0:T(128)S(1)} %exp.90) | copy-start | bytes 292
  16.1 29.9 %copy-start.1 = (f32[6,24,256]{2,1,0:T(8,128)}, f32[6,24,256]{2,1,0:T(8,128)S(1)}, u32[]{:S(2)}) copy-start(f32[6,24,256]{2,1,0:T(8,128)S(1)} %get-tuple-element.1738) | copy-start | bytes 442372
  19.9 26.1 %copy-start.11 = (f32[6,24,2]{1,2,0:T(2,128)}, f32[6,24,2]{1,2,0:T(2,128)S(1)}, u32[]{:S(2)}) copy-start(f32[6,24,2]{1,2,0:T(2,128)S(1)} %slice.164) | copy-start | bytes 3460
  21.2 25.0 %copy-start.6 = (f32[6,256,128]{1,2,0:T(8,128)}, f32[6,256,128]{1,2,0:T(8,128)S(1)}, u32[]{:S(2)}) copy-start(f32[6,256,128]{1,2,0:T(8,128)S(1)} %copy.228) | copy-start | bytes 2359300
  34.1 11.9 %copy-start.10 = (f32[24]{0:T(128)S(1)}, f32[24]{0:T(128)}, u32[]{:S(2)}) copy-start(f32[24]{0:T(128)} %param.26) | copy-start | bytes 292
  45.3 8.9 %copy-start.13 = (f32[6,24]{1,0:T(8,128)}, f32[6,24]{1,0:T(8,128)S(1)}, u32[]{:S(2)}) copy-start(f32[6,24]{1,0:T(8,128)S(1)} %slice_reduce_fusion.7) | copy-start | bytes 1732
  46.0 8.2 %copy-start.19 = (pred[6,256]{1,0:T(8,128)(4,1)}, pred[6,256]{1,0:T(8,128)(4,1)S(1)}, u32[]{:S(2)}) copy-start(pred[6,256]{1,0:T(8,128)(4,1)S(1)} %broadcast_compare_fusion.2) | copy-start | bytes 4612
  150.3 4.4 collective-permute-start
  205.2 8.0 %copy-start.21 = (f32[24]{0:T(128)S(1)}, f32[24]{0:T(128)}, u32[]{:S(2)}) copy-start(f32[24]{0:T(128)} %get-tuple-element.1641) | copy-start | bytes 292 | tf_op jit(solution)/shard_map/transpose(jvp())/while
  205.2 8.0 %copy-start.27 = (f32[24]{0:T(128)S(1)}, f32[24]{0:T(128)}, u32[]{:S(2)}) copy-start(f32[24]{0:T(128)} %get-tuple-element.1642) | copy-start | bytes 292 | tf_op jit(solution)/shard_map/transpose(jvp())/while
  237.8 8.0 %copy-start.21 = (f32[24]{0:T(128)S(1)}, f32[24]{0:T(128)}, u32[]{:S(2)}) copy-start(f32[24]{0:T(128)} %get-tuple-element.1641) | copy-start | bytes 292 | tf_op jit(solution)/shard_map/transpose(jvp())/while
  237.8 8.0 %copy-start.27 = (f32[24]{0:T(128)S(1)}, f32[24]{0:T(128)}, u32[]{:S(2)}) copy-start(f32[24]{0:T(128)} %get-tuple-element.1642) | copy-start | bytes 292 | tf_op jit(solution)/shard_map/transpose(jvp())/while
  270.4 8.0 %copy-start.21 = (f32[24]{0:T(128)S(1)}, f32[24]{0:T(128)}, u32[]{:S(2)}) copy-start(f32[24]{0:T(128)} %get-tuple-element.1641) | copy-start | bytes 292 | tf_op jit(solution)/shard_map/transpose(jvp())/while
  270.4 8.0 %copy-start.27 = (f32[24]{0:T(128)S(1)}, f32[24]{0:T(128)}, u32[]{:S(2)}) copy-start(f32[24]{0:T(128)} %get-tuple-element.1642) | copy-start | bytes 292 | tf_op jit(solution)/shard_map/transpose(jvp())/while
  303.0 8.0 %copy-start.27 = (f32[24]{0:T(128)S(1)}, f32[24]{0:T(128)}, u32[]{:S(2)}) copy-start(f32[24]{0:T(128)} %get-tuple-element.1642) | copy-start | bytes 292 | tf_op jit(solution)/shard_map/transpose(jvp())/while
  335.7 8.0 %copy-start.27 = (f32[24]{0:T(128)S(1)}, f32[24]{0:T(128)}, u32[]{:S(2)}) copy-start(f32[24]{0:T(128)} %get-tuple-element.1642) | copy-start | bytes 292 | tf_op jit(solution)/shard_map/transpose(jvp())/while
  368.3 8.0 %copy-start.21 = (f32[24]{0:T(128)S(1)}, f32[24]{0:T(128)}, u32[]{:S(2)}) copy-start(f32[24]{0:T(128)} %get-tuple-element.1641) | copy-start | bytes 292 | tf_op jit(solution)/shard_map/transpose(jvp())/while
  368.3 8.0 %copy-start.27 = (f32[24]{0:T(128)S(1)}, f32[24]{0:T(128)}, u32[]{:S(2)}) copy-start(f32[24]{0:T(128)} %get-tuple-element.1642) | copy-start | bytes 292 | tf_op jit(solution)/shard_map/transpose(jvp())/while
  377.5 11.6 %copy-start.34 = (f32[24]{0:T(128)S(1)}, f32[24]{0:T(128)}, u32[]{:S(2)}) copy-start(f32[24]{0:T(128)} %broadcast_multiply_fusion) | copy-start | bytes 292
  390.1 4.1 collective-permute-start.1
  394.2 15.2 %copy-start.14 = (f32[6,24]{1,0:T(8,128)S(1)}, f32[6,24]{1,0:T(8,128)}, u32[]{:S(2)}) copy-start(f32[6,24]{1,0:T(8,128)} %copy-done.13) | copy-start | bytes 1732
  394.2 15.2 %copy-start.31 = (pred[6]{0:T(512)(128)(4,1)S(1)}, pred[6]{0:T(512)(128)(4,1)}, u32[]{:S(2)}) copy-start(pred[6]{0:T(512)(128)(4,1)} %copy-done.30) | copy-start | bytes 22
  394.2 16.6 %copy-start.16 = (f32[6,24,256]{2,1,0:T(8,128)S(1)}, f32[6,24,256]{2,1,0:T(8,128)}, u32[]{:S(2)}) copy-start(f32[6,24,256]{2,1,0:T(8,128)} %copy-done.15) | copy-start | bytes 442372
  410.9 23.0 %copy-start.33 = (f32[24]{0:T(128)S(1)}, f32[24]{0:T(128)}, u32[]{:S(2)}) copy-start(f32[24]{0:T(128)} %copy-done.32) | copy-start | bytes 292
  410.9 23.4 %copy-start.9 = (f32[6,24,256]{2,1,0:T(8,128)S(1)}, f32[6,24,256]{2,1,0:T(8,128)}, u32[]{:S(2)}) copy-start(f32[6,24,256]{2,1,0:T(8,128)} %get-tuple-element.772) | copy-start | bytes 442372
  410.9 24.2 %copy-start.3 = (bf16[6,256,256]{1,2,0:T(8,128)(2,1)S(1)}, bf16[6,256,256]{1,2,0:T(8,128)(2,1)}, u32[]{:S(2)}) copy-start(bf16[6,256,256]{1,2,0:T(8,128)(2,1)} %get-tuple-element.771) | copy-start | bytes 2359300
  418.0 18.4 %copy-start.7 = (f32[6,256,128]{1,2,0:T(8,128)S(1)}, f32[6,256,128]{1,2,0:T(8,128)}, u32[]{:S(2)}) copy-start(f32[6,256,128]{1,2,0:T(8,128)} %copy-done.6) | copy-start | bytes 2359300
  453.6 13.1 %copy-start.23 = (f32[24]{0:T(128)S(1)}, f32[24]{0:T(128)}, u32[]{:S(2)}) copy-start(f32[24]{0:T(128)} %get-tuple-element.774) | copy-start | bytes 292
  453.6 13.7 %copy-start.35 = (f32[24]{0:T(128)S(1)}, f32[24]{0:T(128)}, u32[]{:S(2)}) copy-start(f32[24]{0:T(128)} %get-tuple-element.1787) | copy-start | bytes 292
  467.4 62.7 %copy-start.29 = (f32[24]{0:T(128)S(1)}, f32[24]{0:T(128)}, u32[]{:S(2)}) copy-start(f32[24]{0:T(128)} %get-tuple-element.775) | copy-start | bytes 292
  467.4 62.7 %copy-start.26 = (f32[24]{0:T(128)S(1)}, f32[24]{0:T(128)}, u32[]{:S(2)}) copy-start(f32[24]{0:T(128)} %get-tuple-element.776) | copy-start | bytes 292
  (62 other events, 269.2 us)
Sparse Core Ops, SparseCore 0:
  10.8 134.8 all-gather.2
where the time goes:
time: 607 us; the launch traced here: 601 us
  local copies, waits for them, and re-layouts  158 us (26%)
  matrix products  151 us (25%)
  other arithmetic  115 us (19%)
  waiting for transfers between devices  86.9 us (14%)
  blocking collectives  67.2 us (11%)
  between operations  16.4 us (3%)
    all_gather x1, waiting for transfers between devices, shards(): gathered = lax.all_gather(old_states, 'stream', axis=0, tiled=True)  83.2 us
    dot_general x18, matrix products, one_group(): jnp.einsum('hij,jhp->ihp', mixing, inputs_q, preferred_element_type=jnp.f...  81.8 us
    psum x1, blocking collectives, shards(): lax.psum((rates_first + rates_second, bias_first + bias_second, skip_tota...  64.5 us
    another operation x80, other arithmetic  52.5 us
    dot_general x24, matrix products, one_group(): jnp.einsum('in,hpn->ihp', c_part.astype(jnp.float32), starts_q, precision...  43.1 us
    unnamed x56, local copies, waits for them, and re-layouts  35.7 us
    squeeze x30, local copies, waits for them, and re-layouts, outputs(): lax.scan(per_group, 0, (inputs_c, maps_c, logits_c, flags_c, starts_c))  22.8 us
    dot_general x3, matrix products, group_states(): jnp.einsum('cjhp,chjn->chpn', inputs_c, b_weighted, preferred_element_typ...  21.9 us
  transfers between devices with their start and end apart: 3, of which 3 were waited for; matrix products, arithmetic and copies ran while one was open for 9% of the time, Pallas kernels for 0%

commit v1 on v0

--- a/solution.py
+++ b/solution.py
@@ -152,7 +152,8 @@
         (grad_states, grad_decays)
     )
     rates_total, bias_total, skip_sum = lax.psum(
-        (rates_first + rates_second, bias_first + bias_second, skip_total), ("stream", "seq")
+        lax.psum((rates_first + rates_second, bias_first + bias_second, skip_total), "seq"),
+        "stream",
     )
     grad_logits = (logits_first + logits_second).transpose(1, 0, 2).reshape(1, head_count, length)
     return (

time: 607 us -> 721 us (1.19)
  the two profiles are of different devices: /device:TPU:1 before, /device:TPU:0 now
where the time goes in v1:
time: 721 us; the launch traced here: 716 us
  blocking collectives  182 us (25%)
  local copies, waits for them, and re-layouts  158 us (22%)
  matrix products  151 us (21%)
  other arithmetic  115 us (16%)
  waiting for transfers between devices  86.2 us (12%)
  between operations  16.4 us (2%)
    psum x1, blocking collectives, shards(): lax.psum(lax.psum((rates_first + rates_second, bias_first + bias_second,...  177 us
    all_gather x1, waiting for transfers between devices, shards(): gathered = lax.all_gather(old_states, 'stream', axis=0, tiled=True)  82.6 us
    dot_general x18, matrix products, one_group(): jnp.einsum('hij,jhp->ihp', mixing, inputs_q, preferred_element_type=jnp.f...  81.8 us
    another operation x80, other arithmetic  52.5 us
    dot_general x24, matrix products, one_group(): jnp.einsum('in,hpn->ihp', c_part.astype(jnp.float32), starts_q, precision...  43.1 us
    unnamed x56, local copies, waits for them, and re-layouts  35.8 us
    squeeze x30, local copies, waits for them, and re-layouts, outputs(): lax.scan(per_group, 0, (inputs_c, maps_c, logits_c, flags_c, starts_c))  22.8 us
    dot_general x3, matrix products, group_states(): jnp.einsum('cjhp,chjn->chpn', inputs_c, b_weighted, preferred_element_typ...  21.9 us
  transfers between devices with their start and end apart: 3, of which 3 were waited for; matrix products, arithmetic and copies ran while one was open for 7% of the time, Pallas kernels for 0%

profile of v1, /device:TPU:0, one launch (start us, length us, event | category | flops | bytes accessed | tf_op | source)
XLA Modules:
  0.0 715.7 jit_solution(13407831844161415959)
XLA Ops:
  21.2 12.9 %reshape.634 = bf16[6,256,24,64]{3,2,1,0:T(8,128)(2,1)} reshape(bf16[1,1536,1536]{2,1,0:T(8,128)(2,1)} %param.22) | data formatting | bytes 9437184 | tf_op jit(solution)/shard_map/reshape;squeeze | solution.py:107
  34.1 10.3 %copy.231 = bf16[6,256,24,64]{1,3,2,0:T(8,128)(2,1)} copy(bf16[6,256,24,64]{3,2,1,0:T(8,128)(2,1)} %reshape.634) | data formatting | bytes 9437184
  46.2 8.0 %fusion.94 = f32[6,24,64,128]{3,2,1,0:T(8,128)} fusion(bf16[6,256,24,64]{1,3,2,0:T(8,128)(2,1)} %copy.231, f32[6,256,128]{1,2,0:T(8,128)S(1)} %copy.228, f32[6,24,256]{2,1,0:T(8,128)S(1)} %select_multiply_fusion.3), kind=kOutput, calls=%fused_computation.172 | convolution fusion | flops 613416960 | bytes 10371072 | tf_op jit(solution)/shard_map/jvp(cjhp,chjn->chpn)/dot_general | solution.py:31
  54.2 8.0 %while.108 = (s32[]{:T(128)}, f32[24,64,128]{2,1,0:T(8,128)S(1)}, f32[6,24]{1,0:T(8,128)S(1)}, f32[6,24,64,128]{3,2,1,0:T(8,128)}, s32[]{:T(128)}, /*index=5*/s32[]{:T(128)}) while((s32[]{:T(128)}, f32[24,64,128]{2,1,0:T(8,128)S(1)}, f32[6,24]{1,0:T(8,128)S(1)}, f32[6,24,64,128]{3,2,1,0:T(8,128)}, s32[]{:T(128)}, ...), condition=%wide.region_7.8_spmd.clone, body=%wide.region_6.7_spmd.clone.sunk | while | flops 589827 | bytes 2359671 | solution.py:42
  62.3 82.6 %all-gather.3.cloned.1.call-done = f32[64,12,64,128]{3,2,1,0:T(8,128)} async-done(((f32[1,12,64,128]{3,2,1,0:T(8,128)}), f32[64,12,64,128]{3,2,1,0:T(8,128)}) %all-gather.3.cloned.1.call-update) | async-done | bytes 25165840 | tf_op jit(solution)/shard_map/all_gather | solution.py:104
  156.4 17.0 %while.105 = (s32[]{:T(128)}, f32[24,64,128]{2,1,0:T(8,128)S(1)}, f32[6,24,64,128]{3,2,1,0:T(8,128)}, f32[6,24,1,1]{1,3,2,0:T(1,128)}, f32[6,24]{1,0:T(8,128)S(1)}, /*index=5*/f32[6,24,64,128]{3,2,1,0:T(8,128)}, s32[]{:T(128)}) while((s32[]{:T(128)}, f32[24,64,128]{2,1,0:T(8,128)S(1)}, f32[6,24,64,128]{3,2,1,0:T(8,128)}, ...), condition=%wide.region_9.10_spmd, body=%wide.region_8.9_spmd.sunk | while | flops 393218 | bytes 3934165 | solution.py:42
  180.5 195.7 %while.109 = (s32[]{:T(128)}, f32[24]{0:T(128)}, f32[24]{0:T(128)}, f32[24]{0:T(128)}, bf16[6,256,24,64]{1,3,2,0:T(8,128)(2,1)}, /*index=5*/bf16[6,256,256]{1,2,...) while((s32[]{:T(128)}, f32[24]{0:T(128)}, f32[24]{0:T(128)}, ...), condition=%wide.region_31.32_spmd.clone, body=%wide.region_16.31_spmd.clone.sunk | while | flops 2306163200 | bytes 22004424 | solution.py:79
  191.9 6.2 fusion.183
  203.9 3.9 fusion.189
  224.5 6.2 fusion.183
  236.5 3.9 fusion.189
  257.1 6.2 fusion.183
  269.1 3.9 fusion.189
  289.8 6.2 fusion.183
  301.8 3.9 fusion.189
  322.4 6.2 fusion.183
  334.4 3.9 fusion.189
  355.0 6.2 fusion.183
  367.0 3.9 fusion.189
  376.2 11.6 %while.110 = (s32[]{:T(128)}, f32[24,64,128]{2,1,0:T(8,128)S(1)}, f32[6,24,64,128]{3,2,1,0:T(8,128)}, f32[6,24,1,1]{1,3,2,0:T(1,128)}, s32[]{:T(128)}, /*index=5*/s32[]{:T(128)}, s32[]{:T(128)}) while((s32[]{:T(128)}, f32[24,64,128]{2,1,0:T(8,128)S(1)}, f32[6,24,64,128]{3,2,1,0:T(8,128)}, f32[6,24,1,1]{1,3,2,0:T(1,128)}, ...), condition=%wide.region_33.34_spmd.clone, body=%wide.region_32.33_spmd.clone.sunk | while | flops 589828 | bytes 2359691 | solution.py:42
  393.2 15.2 %while.106 = (s32[]{:T(128)}, f32[24,64,128]{2,1,0:T(8,128)S(1)}, bf16[6,24,64,128]{3,2,1,0:T(8,128)(2,1)S(1)}, f32[6,24]{1,0:T(8,128)S(1)}, f32[6,24,64,128]{3,...) while((s32[]{:T(128)}, f32[24,64,128]{2,1,0:T(8,128)S(1)}, ...), condition=%wide.region_36.37_spmd, body=%wide.region_34.36_spmd.sunk | while | flops 786411 | bytes 4719297 | solution.py:42
  409.9 7.1 fusion.87
  417.7 14.9 %reduce-window.130 = f32[6,24,2,128]{3,1,2,0:T(8,128)S(1)} reduce-window(f32[6,24,2,128]{3,1,2,0:T(8,128)S(1)} %copy_bitcast_fusion.5, f32[]{:T(128)} %constant.289.clone.1), window={size=1x1x1x128 pad=0_0x0_0x0_0x0_127}, to_apply=%region_40.41 | reduce-window | flops 4681728 | bytes 294916 | tf_op jit(solution)/shard_map/reduce-window.14
  435.3 6.9 bitcast_add_fusion.6
  442.2 10.4 %copy.250 = bf16[6,256,24,64]{3,2,1,0:T(8,128)(2,1)} copy(bf16[6,256,24,64]{1,3,2,0:T(8,128)(2,1)} %bitcast_add_fusion.6) | data formatting | bytes 9437184
  452.6 13.1 %reshape.633 = bf16[1,1536,1536]{2,1,0:T(8,128)(2,1)} reshape(bf16[6,256,24,64]{3,2,1,0:T(8,128)(2,1)} %copy.250) | data formatting | bytes 9437184
  466.3 62.6 %while.107 = (s32[]{:T(128)}, bf16[6,256,1536]{2,1,0:T(8,128)(2,1)}, bf16[6,256,24,64]{1,3,2,0:T(8,128)(2,1)}, bf16[6,256,256]{2,1,0:T(8,128)(2,1)}, s32[6,256]{...) while((s32[]{:T(128)}, bf16[6,256,1536]{2,1,0:T(8,128)(2,1)}, ...), condition=%wide.region_15.16_spmd.clone, body=%wide.region_10.15_spmd.clone.sunk | while | flops 833433920 | bytes 10981461 | solution.py:79
  472.3 3.5 fusion.167
  492.9 3.6 fusion.167
  513.7 3.6 fusion.167
  524.2 3.5 fusion.167
  531.5 177.4 %all-reduce.5 = (f32[24]{0:T(128)}, f32[24]{0:T(128)}, f32[24]{0:T(128)}) all-reduce(f32[24]{0:T(128)S(1)} %get-tuple-element.1201, f32[24]{0:T(128)S(1)} %get-tuple-element.1202, f32[24]{0:T(128)S(1)} %get-tuple-element.1203), channel_id=1, replica_groups=mesh['stream'=64,'seq'=2] {'stream'}, use_global_device_ids=true, to_apply=%region_44.45 | all-reduce | flops 72 | bytes 576 | tf_op jit(solution)/shard_map/psum | solution.py:154
  (710 shorter events, 278.4 us)
Async XLA Ops:
  7.2 137.7 %all-gather.3.cloned.1.call-start = ((), (), s32[]{:S(2)}) async-start(), calls=%async_computation | async-start | bytes 25559040 | tf_op jit(solution)/shard_map/all_gather | solution.py:104
  14.3 19.8 %copy-start.32 = (f32[24]{0:T(128)}, f32[24]{0:T(128)S(1)}, u32[]{:S(2)}) copy-start(f32[24]{0:T(128)S(1)} %exp.90) | copy-start | bytes 292
  16.1 29.9 %copy-start.1 = (f32[6,24,256]{2,1,0:T(8,128)}, f32[6,24,256]{2,1,0:T(8,128)S(1)}, u32[]{:S(2)}) copy-start(f32[6,24,256]{2,1,0:T(8,128)S(1)} %get-tuple-element.1741) | copy-start | bytes 442372
  19.9 26.1 %copy-start.11 = (f32[6,24,2]{1,2,0:T(2,128)}, f32[6,24,2]{1,2,0:T(2,128)S(1)}, u32[]{:S(2)}) copy-start(f32[6,24,2]{1,2,0:T(2,128)S(1)} %slice.164) | copy-start | bytes 3460
  21.2 25.0 %copy-start.6 = (f32[6,256,128]{1,2,0:T(8,128)}, f32[6,256,128]{1,2,0:T(8,128)S(1)}, u32[]{:S(2)}) copy-start(f32[6,256,128]{1,2,0:T(8,128)S(1)} %copy.228) | copy-start | bytes 2359300
  34.1 11.9 %copy-start.10 = (f32[24]{0:T(128)S(1)}, f32[24]{0:T(128)}, u32[]{:S(2)}) copy-start(f32[24]{0:T(128)} %param.26) | copy-start | bytes 292
  45.3 8.9 %copy-start.13 = (f32[6,24]{1,0:T(8,128)}, f32[6,24]{1,0:T(8,128)S(1)}, u32[]{:S(2)}) copy-start(f32[6,24]{1,0:T(8,128)S(1)} %slice_reduce_fusion.7) | copy-start | bytes 1732
  46.0 8.2 %copy-start.19 = (pred[6,256]{1,0:T(8,128)(4,1)}, pred[6,256]{1,0:T(8,128)(4,1)S(1)}, u32[]{:S(2)}) copy-start(pred[6,256]{1,0:T(8,128)(4,1)S(1)} %broadcast_compare_fusion.2) | copy-start | bytes 4612
  149.3 4.1 collective-permute-start
  203.9 8.0 %copy-start.21 = (f32[24]{0:T(128)S(1)}, f32[24]{0:T(128)}, u32[]{:S(2)}) copy-start(f32[24]{0:T(128)} %get-tuple-element.1644) | copy-start | bytes 292 | tf_op jit(solution)/shard_map/transpose(jvp())/while
  203.9 8.0 %copy-start.27 = (f32[24]{0:T(128)S(1)}, f32[24]{0:T(128)}, u32[]{:S(2)}) copy-start(f32[24]{0:T(128)} %get-tuple-element.1645) | copy-start | bytes 292 | tf_op jit(solution)/shard_map/transpose(jvp())/while
  236.5 8.0 %copy-start.21 = (f32[24]{0:T(128)S(1)}, f32[24]{0:T(128)}, u32[]{:S(2)}) copy-start(f32[24]{0:T(128)} %get-tuple-element.1644) | copy-start | bytes 292 | tf_op jit(solution)/shard_map/transpose(jvp())/while
  236.5 8.0 %copy-start.27 = (f32[24]{0:T(128)S(1)}, f32[24]{0:T(128)}, u32[]{:S(2)}) copy-start(f32[24]{0:T(128)} %get-tuple-element.1645) | copy-start | bytes 292 | tf_op jit(solution)/shard_map/transpose(jvp())/while
  269.1 8.0 %copy-start.21 = (f32[24]{0:T(128)S(1)}, f32[24]{0:T(128)}, u32[]{:S(2)}) copy-start(f32[24]{0:T(128)} %get-tuple-element.1644) | copy-start | bytes 292 | tf_op jit(solution)/shard_map/transpose(jvp())/while
  269.1 8.0 %copy-start.27 = (f32[24]{0:T(128)S(1)}, f32[24]{0:T(128)}, u32[]{:S(2)}) copy-start(f32[24]{0:T(128)} %get-tuple-element.1645) | copy-start | bytes 292 | tf_op jit(solution)/shard_map/transpose(jvp())/while
  301.7 8.0 %copy-start.27 = (f32[24]{0:T(128)S(1)}, f32[24]{0:T(128)}, u32[]{:S(2)}) copy-start(f32[24]{0:T(128)} %get-tuple-element.1645) | copy-start | bytes 292 | tf_op jit(solution)/shard_map/transpose(jvp())/while
  334.4 8.0 %copy-start.27 = (f32[24]{0:T(128)S(1)}, f32[24]{0:T(128)}, u32[]{:S(2)}) copy-start(f32[24]{0:T(128)} %get-tuple-element.1645) | copy-start | bytes 292 | tf_op jit(solution)/shard_map/transpose(jvp())/while
  367.0 8.0 %copy-start.21 = (f32[24]{0:T(128)S(1)}, f32[24]{0:T(128)}, u32[]{:S(2)}) copy-start(f32[24]{0:T(128)} %get-tuple-element.1644) | copy-start | bytes 292 | tf_op jit(solution)/shard_map/transpose(jvp())/while
  367.0 8.0 %copy-start.27 = (f32[24]{0:T(128)S(1)}, f32[24]{0:T(128)}, u32[]{:S(2)}) copy-start(f32[24]{0:T(128)} %get-tuple-element.1645) | copy-start | bytes 292 | tf_op jit(solution)/shard_map/transpose(jvp())/while
  376.2 11.6 %copy-start.34 = (f32[24]{0:T(128)S(1)}, f32[24]{0:T(128)}, u32[]{:S(2)}) copy-start(f32[24]{0:T(128)} %broadcast_multiply_fusion) | copy-start | bytes 292
  388.8 4.4 collective-permute-start.1
  393.2 15.2 %copy-start.14 = (f32[6,24]{1,0:T(8,128)S(1)}, f32[6,24]{1,0:T(8,128)}, u32[]{:S(2)}) copy-start(f32[6,24]{1,0:T(8,128)} %copy-done.13) | copy-start | bytes 1732
  393.2 15.2 %copy-start.31 = (pred[6]{0:T(512)(128)(4,1)S(1)}, pred[6]{0:T(512)(128)(4,1)}, u32[]{:S(2)}) copy-start(pred[6]{0:T(512)(128)(4,1)} %copy-done.30) | copy-start | bytes 22
  393.2 16.6 %copy-start.16 = (f32[6,24,256]{2,1,0:T(8,128)S(1)}, f32[6,24,256]{2,1,0:T(8,128)}, u32[]{:S(2)}) copy-start(f32[6,24,256]{2,1,0:T(8,128)} %copy-done.15) | copy-start | bytes 442372
  409.8 23.0 %copy-start.33 = (f32[24]{0:T(128)S(1)}, f32[24]{0:T(128)}, u32[]{:S(2)}) copy-start(f32[24]{0:T(128)} %copy-done.32) | copy-start | bytes 292
  409.8 23.4 %copy-start.9 = (f32[6,24,256]{2,1,0:T(8,128)S(1)}, f32[6,24,256]{2,1,0:T(8,128)}, u32[]{:S(2)}) copy-start(f32[6,24,256]{2,1,0:T(8,128)} %get-tuple-element.772) | copy-start | bytes 442372
  409.8 24.2 %copy-start.3 = (bf16[6,256,256]{1,2,0:T(8,128)(2,1)S(1)}, bf16[6,256,256]{1,2,0:T(8,128)(2,1)}, u32[]{:S(2)}) copy-start(bf16[6,256,256]{1,2,0:T(8,128)(2,1)} %get-tuple-element.771) | copy-start | bytes 2359300
  416.9 18.4 %copy-start.7 = (f32[6,256,128]{1,2,0:T(8,128)S(1)}, f32[6,256,128]{1,2,0:T(8,128)}, u32[]{:S(2)}) copy-start(f32[6,256,128]{1,2,0:T(8,128)} %copy-done.6) | copy-start | bytes 2359300
  452.6 13.1 %copy-start.23 = (f32[24]{0:T(128)S(1)}, f32[24]{0:T(128)}, u32[]{:S(2)}) copy-start(f32[24]{0:T(128)} %get-tuple-element.774) | copy-start | bytes 292
  452.6 13.7 %copy-start.35 = (f32[24]{0:T(128)S(1)}, f32[24]{0:T(128)}, u32[]{:S(2)}) copy-start(f32[24]{0:T(128)} %get-tuple-element.1790) | copy-start | bytes 292
  466.3 62.7 %copy-start.29 = (f32[24]{0:T(128)S(1)}, f32[24]{0:T(128)}, u32[]{:S(2)}) copy-start(f32[24]{0:T(128)} %get-tuple-element.775) | copy-start | bytes 292
  466.3 62.7 %copy-start.26 = (f32[24]{0:T(128)S(1)}, f32[24]{0:T(128)}, u32[]{:S(2)}) copy-start(f32[24]{0:T(128)} %get-tuple-element.776) | copy-start | bytes 292
  (62 other events, 269.2 us)
Sparse Core Ops, SparseCore 0:
  10.8 134.0 all-gather.2
